TPU v7x, 512 devices: a whole 4x8x8 slice. The times are simulated.
512 devices in a mesh: pages: 16 (over y, core), row: 8 (over z), col: 4 (over x).
Axes of the slice: x: 4, y: 8, z: 8, core: 2. Of those that a mesh axis runs over, the one named last changes fastest.
Arguments:
- residual: bfloat16 [512, 2, 2048], P('pages', None, ('row', 'col')), may hold values from -6 to 6
- fresh_qkv: bfloat16 [512, 2, 3, 2048], P('pages', None, None, 'col'), may hold values from -27 to 27
- prefix_pages: bfloat16 [256, 2, 128, 2048], P('pages', None, 'row', 'col'), may hold values from -6 to 6
- tail_pages: bfloat16 [512, 2, 128, 2048], P('pages', None, 'row', 'col'), may hold values from -6 to 6
- prefix_item: int32 [256], replicated, may hold values from 0 to 255, as said below
- tail_item: int32 [512], replicated, may hold values from 0 to 511, as said below
- prefix_length: int32 [32], replicated, may hold values from 1 to 1024, 20480 in all
- tail_length: int32 [512], replicated, may hold values from 1 to 128, 40960 in all
- out_weight: bfloat16 [2048, 2048], P('col', 'row'), may hold values from -0.125 to 0.125
- out_bias: bfloat16 [2048], P(('row', 'col')), may hold values from -4 to 4
- mlp_gain: bfloat16 [2048], P('row'), may hold values from 0.25 to 1.75
- mlp_shift: bfloat16 [2048], P('row'), may hold values from -4 to 4
- up_weight: bfloat16 [2048, 8192], P('row', 'col'), may hold values from -0.125 to 0.125
- up_bias: bfloat16 [8192], P(('col', 'row')), may hold values from -4 to 4
- down_weight: bfloat16 [8192, 2048], P('col', 'row'), may hold values from -0.0625 to 0.0625
- down_bias: bfloat16 [2048], P(('row', 'col')), may hold values from -4 to 4
- next_gain: bfloat16 [2048], P('row'), may hold values from 0.25 to 1.75
- next_shift: bfloat16 [2048], P('row'), may hold values from -4 to 4
- score_weight: bfloat16 [2048], P('row'), may hold values from -0.125 to 0.125
- qkv_weight: bfloat16 [2048, 6144], P('row', 'col'), may hold values from -0.125 to 0.125
- qkv_bias: bfloat16 [6144], P(('col', 'row')), may hold values from -4 to 4
Outputs:
- layer_out: bfloat16 [512, 2, 2048], P('pages', None, ('row', 'col'))
- score_out: float32 [512, 2], P('pages')
- projected_next: bfloat16 [512, 2, 6144], P('pages', None, ('col', 'row'))
Inputs may be any that keep to these rules, and one draw needn't show every extreme that they name: `prefix_item`: each of the 256 prompt pages is held by exactly one slot; slot h * 16 + g + k (k < 1) holds a page of one of the prompts g * 2 to (g + 1) * 2 - 1. `tail_item`: each continuation's tail is held by exactly one slot; slot h * 32 + g * 2 + k (k < 2) holds the tail of one of the continuations g * 32 to (g + 1) * 32 - 1. `prefix_length`: some prompt has exactly 1024 cached tokens. `tail_length`: some continuation has exactly 128 tail tokens.
All inputs are finite; a program needn't handle non-finite values.
Results may differ from a plain program's by a relative error of at most 0.023.
Values may be sent and summed in bfloat16 or wider, within the bound.
No kernel may reach another device: no remote copies, remote signals or barrier semaphores. Data moves between devices by JAX's collectives and lax.ppermute only.
A program may use at most 64 MiB of HBM per device.

v0:
```python
import math
import jax
import jax.numpy as jnp
from jax import lax
from jax.sharding import PartitionSpec as P

D = 2048
H = 16
HD = 128
PAGE = 128
MAXPAGES = 8
CONT = 16
masked_score = -1e30
norm_eps = 1e-05


def combined_all(shard, axis, combine):
    everything = jax.tree.map(lambda part: lax.all_gather(part, axis), shard)
    first = jax.tree.map(lambda part: part[0], everything)

    def step(k, so_far):
        return combine(so_far, jax.tree.map(lambda part: part[k], everything))

    return lax.fori_loop(1, lax.axis_size(axis), step, first)


def head_slopes(first_head, how_many):
    head_index = first_head + jnp.arange(how_many, dtype=jnp.int32)
    return jnp.exp2(-8.0 * (head_index + 1).astype(jnp.float32) / H)


def slot_partials(queries, page_keys, page_values, usable, offset, slopes):
    scores = jnp.einsum(
        "sqhd,skhd->sqhk", queries, page_keys, preferred_element_type=jnp.float32
    ) / math.sqrt(HD)
    scores = scores + slopes[None, None, :, None] * offset[:, :, None, :]
    usable_full = usable[:, :, None, :]
    scores = jnp.where(usable_full, scores, masked_score)
    maxima = jnp.max(scores, axis=3)
    weights = jnp.where(usable_full, jnp.exp(scores - maxima[..., None]), 0.0)
    totals = jnp.sum(weights, axis=3)
    outputs = jnp.einsum(
        "sqhk,skhd->sqhd", weights, page_values.astype(jnp.float32), precision=lax.Precision.HIGHEST
    )
    return (maxima, totals, outputs)


def merge_pair(left_part, right_part):
    left_max, left_total, left_out = left_part
    right_max, right_total, right_out = right_part
    joined = jnp.maximum(left_max, right_max)
    left_scale = jnp.exp(left_max - joined)
    right_scale = jnp.exp(right_max - joined)
    return (
        joined,
        left_scale * left_total + right_scale * right_total,
        left_scale[..., None] * left_out + right_scale[..., None] * right_out,
    )


def fold_sources(maxima, totals, outputs):
    joined = jnp.max(maxima, axis=0)
    rescale = jnp.exp(maxima - joined[None])
    return (
        joined,
        jnp.sum(rescale * totals, axis=0),
        jnp.sum(rescale[..., None] * outputs, axis=0),
    )


def cache_partials(
    queries,
    page_block,
    page_item,
    tail_block,
    tail_owner,
    prefix_length,
    tail_length,
    row_index,
    slopes,
):
    cont_count = queries.shape[0]
    prompts = cont_count // CONT
    head_count = queries.shape[2]
    slot_count = page_block.shape[0]
    tokens = page_block.shape[2]
    token_index = row_index * tokens + jnp.arange(tokens, dtype=jnp.int32)
    step_index = jnp.arange(2, dtype=jnp.int32)
    slot_prompt = page_item // MAXPAGES
    slot_page = page_item % MAXPAGES
    by_prompt = queries.reshape(prompts, CONT * 2, head_count, HD)
    key_pos = slot_page[:, None] * PAGE + token_index[None, :]
    slot_len = prefix_length[slot_prompt]
    slot_tails = tail_length.reshape(prompts, CONT)[slot_prompt]
    query_pos = (
        slot_len[:, None, None] + slot_tails[:, :, None] + step_index[None, None, :]
    ).reshape(slot_count, CONT * 2)
    offset = (key_pos[:, None, :] - query_pos[:, :, None]).astype(jnp.float32)
    usable = jnp.broadcast_to((key_pos < slot_len[:, None])[:, None, :], offset.shape)
    page_keys = page_block[:, 0].reshape(slot_count, tokens, head_count, HD)
    page_values = page_block[:, 1].reshape(slot_count, tokens, head_count, HD)
    maxima, totals, outputs = slot_partials(
        by_prompt[slot_prompt], page_keys, page_values, usable, offset, slopes
    )
    prompt_max = (
        jnp.full((prompts, CONT * 2, head_count), masked_score, jnp.float32)
        .at[slot_prompt]
        .max(maxima)
    )
    rescale = jnp.exp(maxima - prompt_max[slot_prompt])
    prompt_total = (
        jnp.zeros((prompts, CONT * 2, head_count), jnp.float32)
        .at[slot_prompt]
        .add(rescale * totals)
    )
    prompt_out = (
        jnp.zeros((prompts, CONT * 2, head_count, HD), jnp.float32)
        .at[slot_prompt]
        .add(rescale[..., None] * outputs)
    )
    prefix_part = (
        prompt_max.reshape(cont_count, 2, head_count),
        prompt_total.reshape(cont_count, 2, head_count),
        prompt_out.reshape(cont_count, 2, head_count, HD),
    )
    tail_count = tail_block.shape[0]
    tail_lens = tail_length[tail_owner]
    tail_usable = jnp.broadcast_to(
        (token_index[None, :] < tail_lens[:, None])[:, None, :], (tail_count, 2, tokens)
    )
    tail_offset = (
        token_index[None, None, :] - tail_lens[:, None, None] - step_index[None, :, None]
    ).astype(jnp.float32)
    tail_keys = tail_block[:, 0].reshape(tail_count, tokens, head_count, HD)
    tail_values = tail_block[:, 1].reshape(tail_count, tokens, head_count, HD)
    tail_max, tail_total, tail_out = slot_partials(
        queries[tail_owner], tail_keys, tail_values, tail_usable, tail_offset, slopes
    )
    cont_max = (
        jnp.full((cont_count, 2, head_count), masked_score, jnp.float32)
        .at[tail_owner]
        .set(tail_max)
    )
    cont_total = jnp.zeros((cont_count, 2, head_count), jnp.float32).at[tail_owner].set(tail_total)
    cont_out = jnp.zeros((cont_count, 2, head_count, HD), jnp.float32).at[tail_owner].set(tail_out)
    return merge_pair(prefix_part, (cont_max, cont_total, cont_out))


def normalize(values, sum_one, sum_two, gain, shift):
    center = sum_one / D
    spread = sum_two / D - center * center
    return (
        (values - center[:, None])
        * lax.rsqrt(spread + norm_eps)[:, None]
        * gain.astype(jnp.float32)
        + shift.astype(jnp.float32)
    ).astype(jnp.bfloat16)


def shards(
    residual,
    fresh_qkv,
    prefix_pages,
    tail_pages,
    prefix_item,
    tail_item,
    prefix_length,
    tail_length,
    out_weight,
    out_bias,
    mlp_gain,
    mlp_shift,
    up_weight,
    up_bias,
    down_weight,
    down_bias,
    next_gain,
    next_shift,
    score_weight,
    qkv_weight,
    qkv_bias,
):
    group_index = lax.axis_index("pages")
    row_index = lax.axis_index("row")
    col_index = lax.axis_index("col")
    group_count = lax.axis_size("pages")
    cont_local = residual.shape[0]
    row_total = cont_local * 2
    share = residual.shape[2]
    head_count = fresh_qkv.shape[3] // HD
    slopes = head_slopes(col_index * head_count, head_count)
    fresh_rows = fresh_qkv.reshape(cont_local, 2, 3, head_count, HD)
    slot_count = prefix_pages.shape[0]
    tail_slots = tail_pages.shape[0]
    everyone = lax.all_gather(fresh_qkv[:, :, 0], "pages", axis=0, tiled=True)
    page_item = lax.dynamic_slice_in_dim(prefix_item, group_index * slot_count, slot_count)
    tail_owner = lax.dynamic_slice_in_dim(tail_item, group_index * tail_slots, tail_slots)
    maxima, totals, outputs = cache_partials(
        everyone.reshape(everyone.shape[0], 2, head_count, HD),
        prefix_pages,
        page_item,
        tail_pages,
        tail_owner,
        prefix_length,
        tail_length,
        row_index,
        slopes,
    )
    maxima, totals, outputs = (
        lax.all_to_all(
            maxima.reshape(group_count, row_total, head_count),
            "pages",
            split_axis=0,
            concat_axis=0,
            tiled=True,
        ),
        lax.all_to_all(
            totals.reshape(group_count, row_total, head_count),
            "pages",
            split_axis=0,
            concat_axis=0,
            tiled=True,
        ),
        lax.all_to_all(
            outputs.reshape(group_count, row_total, head_count, HD),
            "pages",
            split_axis=0,
            concat_axis=0,
            tiled=True,
        ),
    )
    cache_max, cache_total, cache_out = fold_sources(maxima, totals, outputs)
    cache_max, cache_total, cache_out = combined_all(
        (cache_max, cache_total, cache_out), "row", merge_pair
    )
    step_index = jnp.arange(2, dtype=jnp.int32)
    new_usable = jnp.broadcast_to(
        (step_index[None, :] <= step_index[:, None])[None], (cont_local, 2, 2)
    )
    new_offset = jnp.broadcast_to(
        (step_index[None, :] - step_index[:, None]).astype(jnp.float32)[None], (cont_local, 2, 2)
    )
    new_part = slot_partials(
        fresh_rows[:, :, 0],
        fresh_rows[:, :, 1],
        fresh_rows[:, :, 2],
        new_usable,
        new_offset,
        slopes,
    )
    joined_max, joined_total, joined_out = merge_pair(
        (
            cache_max.reshape(cont_local, 2, head_count),
            cache_total.reshape(cont_local, 2, head_count),
            cache_out.reshape(cont_local, 2, head_count, HD),
        ),
        new_part,
    )
    attended = (
        (joined_out / joined_total[..., None])
        .astype(jnp.bfloat16)
        .reshape(row_total, head_count * HD)
    )
    head_term = jnp.dot(attended, out_weight, preferred_element_type=jnp.float32)
    hidden_one = (
        residual.reshape(row_total, share).astype(jnp.float32)
        + lax.psum_scatter(head_term, "col", scatter_dimension=1, tiled=True)
        + out_bias.astype(jnp.float32)
    )
    gain_part = lax.dynamic_slice_in_dim(mlp_gain, col_index * share, share)
    shift_part = lax.dynamic_slice_in_dim(mlp_shift, col_index * share, share)
    sum_one, sum_two = lax.psum(
        (jnp.sum(hidden_one, axis=1), jnp.sum(hidden_one * hidden_one, axis=1)), ("row", "col")
    )
    normed_a = lax.all_gather(
        normalize(hidden_one, sum_one, sum_two, gain_part, shift_part), "col", axis=1, tiled=True
    )
    up_share = lax.psum_scatter(
        jnp.dot(normed_a, up_weight, preferred_element_type=jnp.float32),
        "row",
        scatter_dimension=1,
        tiled=True,
    )
    hidden_two = jax.nn.gelu(up_share + up_bias.astype(jnp.float32), approximate=True).astype(
        jnp.bfloat16
    )
    down_sum = jnp.dot(
        lax.all_gather(hidden_two, "row", axis=1, tiled=True),
        down_weight,
        preferred_element_type=jnp.float32,
    )
    down_share = lax.psum_scatter(
        down_sum.astype(jnp.bfloat16), "col", scatter_dimension=1, tiled=True
    ).astype(jnp.float32)
    layer_out = (hidden_one + down_share + down_bias.astype(jnp.float32)).astype(jnp.bfloat16)
    out_wide = layer_out.astype(jnp.float32)
    gain_part = lax.dynamic_slice_in_dim(next_gain, col_index * share, share)
    shift_part = lax.dynamic_slice_in_dim(next_shift, col_index * share, share)
    score_part = lax.dynamic_slice_in_dim(score_weight, col_index * share, share).astype(
        jnp.float32
    )
    sum_one, sum_two, score_sum = lax.psum(
        (
            jnp.sum(out_wide, axis=1),
            jnp.sum(out_wide * out_wide, axis=1),
            jnp.sum(out_wide * score_part, axis=1),
        ),
        ("row", "col"),
    )
    normed_b = lax.all_gather(
        normalize(out_wide, sum_one, sum_two, gain_part, shift_part), "col", axis=1, tiled=True
    )
    qkv_share = lax.psum_scatter(
        jnp.dot(normed_b, qkv_weight, preferred_element_type=jnp.float32).astype(jnp.bfloat16),
        "row",
        scatter_dimension=1,
        tiled=True,
    ).astype(jnp.float32)
    projected_next = (qkv_share + qkv_bias.astype(jnp.float32)).astype(jnp.bfloat16)
    return (
        layer_out.reshape(cont_local, 2, share),
        score_sum.reshape(cont_local, 2),
        projected_next.reshape(cont_local, 2, qkv_share.shape[1]),
    )


def solution(mesh):
    in_specs = (
        P("pages", None, ("row", "col")),
        P("pages", None, None, "col"),
        P("pages", None, "row", "col"),
        P("pages", None, "row", "col"),
        P(),
        P(),
        P(),
        P(),
        P("col", "row"),
        P(("row", "col")),
        P("row"),
        P("row"),
        P("row", "col"),
        P(("col", "row")),
        P("col", "row"),
        P(("row", "col")),
        P("row"),
        P("row"),
        P("row"),
        P("row", "col"),
        P(("col", "row")),
    )
    out_specs = (
        P("pages", None, ("row", "col")),
        P("pages", None),
        P("pages", None, ("col", "row")),
    )
    return jax.shard_map(shards, mesh=mesh, in_specs=in_specs, out_specs=out_specs, check_vma=False)
```

profile of v0, /device:TPU:2, one launch (start us, length us, event | category | flops | bytes accessed | tf_op | source)
XLA Modules:
  0.0 629.2 jit_solution(3406723916201025579)
XLA Ops:
  19.9 35.8 %all-gather.9.cloned.1.call-done = bf16[512,2,1,512]{3,1,2,0:T(2,128)(2,1)} async-done(((bf16[32,2,1,512]{3,1,2,0:T(2,128)(2,1)}), bf16[512,2,1,512]{3,1,2,0:T(2,128)(2,1)}) %all-gather.9.cloned.1.call-update) | async-done | bytes 1048592 | tf_op jit(solution)/shard_map/all_gather | solution.py:195
  55.7 1.7 reshape_reshape.3
  64.1 2.0 gather_fusion.4
  75.7 2.5 multiply_add_fusion
  80.2 4.6 all-to-all-start
  84.8 2.9 fusion.4
  89.6 2.6 scatter_fusion.4
  96.0 7.2 %all-to-all-start.1 = ((f32[16,1,256]{2,1,0:T(1,128)}), f32[16,1,256]{2,1,0:T(1,128)S(1)}, u32[]{:S(2)}, u32[]{:S(2)}) async-start(f32[16,1,256]{2,1,0:T(1,128)} %reshape.385), calls=%async_computation.1 | async-start | bytes 32768 | tf_op jit(solution)/shard_map/all_to_all | solution.py:217
  103.2 6.1 fusion.3
  110.8 5.7 all-to-all-start.2
  119.8 45.9 %all-to-all-done.2 = f32[16,64,4,128]{3,2,1,0:T(4,128)S(1)} async-done(((f32[16,64,4,128]{3,2,1,0:T(4,128)}), f32[16,64,4,128]{3,2,1,0:T(4,128)S(1)}, u32[]{:S(2)}, u32[]{:S(2)}) %all-to-all-start.2) | async-done | bytes 2097184 | tf_op jit(solution)/shard_map/all_to_all | solution.py:224
  165.7 2.9 multiply_reduce_fusion
  170.9 24.3 %all-gather.4 = f32[8,64,4]{1,2,0:T(4,128)S(1)} all-gather(f32[1,64,4]{1,2,0:T(4,128)S(1)} %copy.149), channel_id=3, replica_groups=mesh['pages'=16,'row'=8,'col'=4] {'row'}, dimensions={0}, use_global_device_ids=true | all-gather | bytes 9216 | tf_op jit(solution)/shard_map/all_gather | solution.py:18
  195.2 21.2 %all-gather.5 = f32[8,64,4]{1,2,0:T(4,128)S(1)} all-gather(f32[1,64,4]{1,2,0:T(4,128)S(1)} %copy.155), channel_id=4, replica_groups=mesh['pages'=16,'row'=8,'col'=4] {'row'}, dimensions={0}, use_global_device_ids=true | all-gather | bytes 9216 | tf_op jit(solution)/shard_map/all_gather | solution.py:18
  217.3 10.9 %while.19 = (s32[]{:T(128)}, f32[64,4]{0,1:T(4,128)S(1)}, f32[64,4]{0,1:T(4,128)S(1)}, f32[64,4,128]{2,1,0:T(4,128)S(1)}, f32[8,64,4]{1,2,0:T(4,128)S(1)}, /*ind...) while((s32[]{:T(128)}, f32[64,4]{0,1:T(4,128)S(1)}, ...), condition=%wide.region_14.15_spmd, body=%wide.region_13.14_spmd.sunk | while | flops 99845 | bytes 407703 | solution.py:24
  230.1 20.7 %reduce-scatter.13.cloned.1.call-done = f32[64,64]{1,0:T(8,128)} async-done(((f32[256,64]{1,0:T(8,128)}), f32[64,64]{1,0:T(8,128)}) %reduce-scatter.13.cloned.1.call-update) | async-done | bytes 16400
  251.7 71.3 %all-reduce.1 = (f32[64]{0:T(128)S(1)}, f32[64]{0:T(128)S(1)}) all-reduce(f32[64]{0:T(128)S(1)} %get-tuple-element.200, f32[64]{0:T(128)S(1)} %get-tuple-element.199), channel_id=1, replica_groups=mesh['pages'=16,'row'=8,'col'=4] {'row','col'}, use_global_device_ids=true, to_apply=%region_21.22 | all-reduce | flops 128 | bytes 1024 | tf_op jit(solution)/shard_map/psum | solution.py:272
  323.2 12.8 %all_gather.37 = bf16[64,256]{0,1:T(8,128)(2,1)S(1)} all-gather(bf16[64,64]{0,1:T(8,128)(2,1)S(1)} %copy.179), channel_id=1, replica_groups=mesh['pages'=16,'row'=8,'col'=4] {'col'}, dimensions={1}, use_global_device_ids=true | all-gather | bytes 40960 | tf_op jit(solution)/shard_map/all_gather | solution.py:275
  337.4 39.7 %reduce-scatter.11.cloned.1.call-done = f32[64,256]{1,0:T(8,128)} async-done(((f32[64,2048]{1,0:T(8,128)}), f32[64,256]{1,0:T(8,128)}) %reduce-scatter.11.cloned.1.call-update) | async-done | bytes 65552 | tf_op jit(solution)/shard_map/reduce_scatter | solution.py:278
  378.0 24.8 %all_gather.38 = bf16[64,2048]{1,0:T(8,128)(2,1)S(1)} all-gather(bf16[64,256]{1,0:T(8,128)(2,1)S(1)} %fusion.32), channel_id=1, replica_groups=mesh['pages'=16,'row'=8,'col'=4] {'row'}, dimensions={1}, use_global_device_ids=true | all-gather | bytes 294912 | tf_op jit(solution)/shard_map/all_gather | solution.py:288
  403.9 22.6 %reduce-scatter.15.cloned.1.call-done = bf16[64,64]{1,0:T(8,128)(2,1)} async-done(((bf16[256,64]{1,0:T(8,128)(2,1)}), bf16[64,64]{1,0:T(8,128)(2,1)}) %reduce-scatter.15.cloned.1.call-update) | async-done | bytes 8208
  427.6 138.0 %all-reduce = (f32[32,2]{1,0:T(8,128)S(1)}, f32[64]{0:T(128)S(1)}, f32[64]{0:T(128)S(1)}) all-reduce(f32[32,2]{1,0:T(8,128)S(1)} %reshape.245, f32[64]{0:T(128)S(1)} %get-tuple-element.202, f32[64]{0:T(128)S(1)} %get-tuple-element.201), channel_id=1, replica_groups=mesh['pages'=16,'row'=8,'col'=4] {'row','col'}, use_global_device_ids=true, to_apply=%region_25.26 | all-reduce | flops 192 | bytes 1536 | tf_op jit(solution)/shard_map/psum | solution.py:302
  565.8 14.2 %all_gather.39 = bf16[64,256]{0,1:T(8,128)(2,1)S(1)} all-gather(bf16[64,64]{0,1:T(8,128)(2,1)S(1)} %copy.180), channel_id=1, replica_groups=mesh['pages'=16,'row'=8,'col'=4] {'col'}, dimensions={1}, use_global_device_ids=true | all-gather | bytes 40960 | tf_op jit(solution)/shard_map/all_gather | solution.py:310
  581.9 38.9 %reduce-scatter.17.cloned.1.call-done = bf16[192,64]{1,0:T(8,128)(2,1)} async-done(((bf16[1536,64]{1,0:T(8,128)(2,1)}), bf16[192,64]{1,0:T(8,128)(2,1)}) %reduce-scatter.17.cloned.1.call-update) | async-done | bytes 24592
  (237 shorter events, 65.7 us)
Async XLA Ops:
  7.2 328.9 %copy-start = (bf16[256,2048]{1,0:T(8,128)(2,1)S(1)}, bf16[256,2048]{1,0:T(8,128)(2,1)}, u32[]{:S(2)}) copy-start(bf16[256,2048]{1,0:T(8,128)(2,1)} %param.35) | copy-start | bytes 3145732
  7.2 48.5 %all-gather.9.cloned.1.call-start = ((), (), s32[]{:S(2)}) async-start(), calls=%async_computation.8 | async-start | bytes 1114112 | tf_op jit(solution)/shard_map/all_gather | solution.py:195
  14.8 55.5 %copy-start.19 = (s32[16]{0:T(128)}, s32[16]{0:T(128)S(1)}, u32[]{:S(2)}) copy-start(s32[16]{0:T(128)S(1)} %compare_select_fusion.1) | copy-start | bytes 196
  18.9 50.4 %copy-start.16 = (pred[16,16]{1,0:T(8,128)(4,1)}, pred[16,16]{1,0:T(8,128)(4,1)S(1)}, u32[]{:S(2)}) copy-start(pred[16,16]{1,0:T(8,128)(4,1)S(1)} %broadcast_compare_fusion.1) | copy-start | bytes 772
  80.2 15.7 %all-to-all-start = ((f32[16,1,256]{2,1,0:T(1,128)}), f32[16,1,256]{2,1,0:T(1,128)S(1)}, u32[]{:S(2)}, u32[]{:S(2)}) async-start(f32[16,1,256]{2,1,0:T(1,128)} %reshape.383), calls=%async_computation | async-start | bytes 32768 | tf_op jit(solution)/shard_map/all_to_all | solution.py:210
  96.0 14.9 %all-to-all-start.1 = ((f32[16,1,256]{2,1,0:T(1,128)}), f32[16,1,256]{2,1,0:T(1,128)S(1)}, u32[]{:S(2)}, u32[]{:S(2)}) async-start(f32[16,1,256]{2,1,0:T(1,128)} %reshape.385), calls=%async_computation.1 | async-start | bytes 32768 | tf_op jit(solution)/shard_map/all_to_all | solution.py:217
  110.8 54.9 %all-to-all-start.2 = ((f32[16,64,4,128]{3,2,1,0:T(4,128)}), f32[16,64,4,128]{3,2,1,0:T(4,128)S(1)}, u32[]{:S(2)}, u32[]{:S(2)}) async-start(f32[16,64,4,128]{3,2,1,0:T(4,128)} %bitcast.145), calls=%async_computation.2 | async-start | bytes 4194304 | tf_op jit(solution)/shard_map/all_to_all | solution.py:224
  116.5 52.1 %copy-start.8 = (bf16[32,2,3,512]{3,1,2,0:T(2,128)(2,1)S(1)}, bf16[32,2,3,512]{3,1,2,0:T(2,128)(2,1)}, u32[]{:S(2)}) copy-start(bf16[32,2,3,512]{3,1,2,0:T(2,128)(2,1)} %param.24) | copy-start | bytes 589828
  116.5 99.8 %all-gather.11.cloned.1.call-start = ((), (), s32[]{:S(2)}) async-start(), calls=%async_computation.9 | async-start | bytes 1179648 | tf_op jit(solution)/shard_map/all_gather | solution.py:18
  118.7 50.2 %copy-start.35 = (f32[4]{0:T(128)S(1)}, f32[4]{0:T(128)}, u32[]{:S(2)}) copy-start(f32[4]{0:T(128)} %multiply_exponential_fusion) | copy-start | bytes 52
  168.6 82.1 %reduce-scatter.13.cloned.1.call-start = ((), (), s32[]{:S(2)}) async-start(), calls=%async_computation.10 | async-start | bytes 163840
  170.5 58.4 %copy-start.9 = (bf16[512,256]{1,0:T(8,128)(2,1)S(1)}, bf16[512,256]{1,0:T(8,128)(2,1)}, u32[]{:S(2)}) copy-start(bf16[512,256]{1,0:T(8,128)(2,1)} %param.31) | copy-start | bytes 786436
  228.3 109.0 %copy-start.31 = (bf16[64]{0:T(256)(128)(2,1)S(1)}, bf16[64]{0:T(256)(128)(2,1)}, u32[]{:S(2)}) copy-start(bf16[64]{0:T(256)(128)(2,1)} %param.38) | copy-start | bytes 388
  228.3 109.0 %copy-start.32 = (bf16[256]{0:T(256)(128)(2,1)S(1)}, bf16[256]{0:T(256)(128)(2,1)}, u32[]{:S(2)}) copy-start(bf16[256]{0:T(256)(128)(2,1)} %param.36) | copy-start | bytes 1540
  228.3 109.0 %copy-start.28 = (bf16[256]{0:T(256)(128)(2,1)S(1)}, bf16[256]{0:T(256)(128)(2,1)}, u32[]{:S(2)}) copy-start(bf16[256]{0:T(256)(128)(2,1)} %param.40) | copy-start | bytes 1540
  228.3 109.0 %copy-start.29 = (bf16[256]{0:T(256)(128)(2,1)S(1)}, bf16[256]{0:T(256)(128)(2,1)}, u32[]{:S(2)}) copy-start(bf16[256]{0:T(256)(128)(2,1)} %param.39) | copy-start | bytes 1540
  228.3 174.5 %copy-start.4 = (bf16[2048,256]{1,0:T(8,128)(2,1)S(1)}, bf16[2048,256]{1,0:T(8,128)(2,1)}, u32[]{:S(2)}) copy-start(bf16[2048,256]{1,0:T(8,128)(2,1)} %param.37) | copy-start | bytes 3145732
  229.9 147.2 %reduce-scatter.11.cloned.1.call-start = ((), (), s32[]{:S(2)}) async-start(), calls=%async_computation.7 | async-start | bytes 589824 | tf_op jit(solution)/shard_map/reduce_scatter | solution.py:278
  323.1 80.7 %copy-start.33 = (bf16[256]{0:T(256)(128)(2,1)S(1)}, bf16[256]{0:T(256)(128)(2,1)}, u32[]{:S(2)}) copy-start(bf16[256]{0:T(256)(128)(2,1)} %param.41) | copy-start | bytes 1540
  336.1 244.0 %copy-start.5 = (bf16[256,1536]{1,0:T(8,128)(2,1)S(1)}, bf16[256,1536]{1,0:T(8,128)(2,1)}, u32[]{:S(2)}) copy-start(bf16[256,1536]{1,0:T(8,128)(2,1)} %param.42) | copy-start | bytes 2359300
  337.2 89.3 %reduce-scatter.15.cloned.1.call-start = ((), (), s32[]{:S(2)}) async-start(), calls=%async_computation.11 | async-start | bytes 81920
  377.9 203.3 %copy-start.34 = (bf16[192]{0:T(256)(128)(2,1)S(1)}, bf16[192]{0:T(256)(128)(2,1)}, u32[]{:S(2)}) copy-start(bf16[192]{0:T(256)(128)(2,1)} %param.43) | copy-start | bytes 1156
  403.8 217.0 %reduce-scatter.17.cloned.1.call-start = ((), (), s32[]{:S(2)}) async-start(), calls=%async_computation.12 | async-start | bytes 442368
  427.5 194.9 %copy-start.15 = (bf16[64,64]{1,0:T(8,128)(2,1)}, bf16[64,64]{1,0:T(8,128)(2,1)S(1)}, u32[]{:S(2)}) copy-start(bf16[64,64]{1,0:T(8,128)(2,1)S(1)} %get-tuple-element.227) | copy-start | bytes 24580
  (21 other events, 209.7 us)
Sparse Core Ops, SparseCore 0:
  10.2 45.5 all-gather.8
  168.7 41.4 all-gather.10
  230.0 20.6 reduce-scatter.12
  337.3 39.6 reduce-scatter.10
  403.9 22.5 reduce-scatter.14
  581.4 39.4 reduce-scatter.16
where the time goes:
time: 630 us; the launch traced here: 629 us
  blocking collectives  307 us (49%)
  waiting for transfers between devices  205 us (33%)
  local copies, waits for them, and re-layouts  40.9 us (6%)
  other arithmetic  33.2 us (5%)
  starting transfers between devices  17.7 us (3%)
  between operations  14.9 us (2%)
  matrix products  10.4 us (2%)
    psum x1, blocking collectives, shards(): lax.psum((jnp.sum(out_wide, axis=1), jnp.sum(out_wide * out_wide, axis=1)...  138 us
    unnamed x9, waiting for transfers between devices  82.3 us
    psum x1, blocking collectives, shards(): lax.psum((jnp.sum(hidden_one, axis=1), jnp.sum(hidden_one * hidden_one, a...  71.3 us
    all_to_all x1, waiting for transfers between devices, shards(): lax.all_to_all(outputs.reshape(group_count, row_total, head_count, HD), '...  45.9 us
    all_gather x2, blocking collectives, combined_all(): everything = jax.tree.map(lambda part: lax.all_gather(part, axis), shard)  45.5 us
    reduce_scatter x1, waiting for transfers between devices, shards(): lax.psum_scatter(jnp.dot(normed_a, up_weight, preferred_element_type=jnp....  39.7 us
    all_gather x1, waiting for transfers between devices, shards(): everyone = lax.all_gather(fresh_qkv[:, :, 0], 'pages', axis=0, tiled=True)  35.8 us
    all_gather x1, blocking collectives, shards(): lax.all_gather(hidden_two, 'row', axis=1, tiled=True)  24.8 us
  transfers between devices with their start and end apart: 9, of which 7 were waited for; matrix products, arithmetic and copies ran while one was open for 5% of the time, Pallas kernels for 0%

commit v1 on v0

--- a/solution.py
+++ b/solution.py
@@ -270,7 +270,8 @@
     gain_part = lax.dynamic_slice_in_dim(mlp_gain, col_index * share, share)
     shift_part = lax.dynamic_slice_in_dim(mlp_shift, col_index * share, share)
     sum_one, sum_two = lax.psum(
-        (jnp.sum(hidden_one, axis=1), jnp.sum(hidden_one * hidden_one, axis=1)), ("row", "col")
+        lax.psum((jnp.sum(hidden_one, axis=1), jnp.sum(hidden_one * hidden_one, axis=1)), "col"),
+        "row",
     )
     normed_a = lax.all_gather(
         normalize(hidden_one, sum_one, sum_two, gain_part, shift_part), "col", axis=1, tiled=True

time: 630 us -> 584 us (0.927)
  blocking collectives: 307 us -> 261 us
    psum x1, blocking collectives: 71.3 us -> 9.38 us  [shards(): lax.psum((jnp.sum(hidden_one, axis=1), jnp.sum(hidden_one * hidden_one, a...]
    psum x0 -> x1, blocking collectives: none -> 18.1 us  [shards(): lax.psum(lax.psum((jnp.sum(hidden_one, axis=1), jnp.sum(hidden_one * hidd...]
  transfers between devices with their start and end apart: 9 -> 9, of which waited for: 7 -> 7; matrix products, arithmetic and copies ran while one was open for 5% -> 6% of each run, Pallas kernels for 0% -> 0%
where the time goes in v1:
time: 584 us; the launch traced here: 582 us
  blocking collectives  261 us (45%)
  waiting for transfers between devices  204 us (35%)
  local copies, waits for them, and re-layouts  40.9 us (7%)
  other arithmetic  33.2 us (6%)
  starting transfers between devices  17.7 us (3%)
  between operations  14.9 us (3%)
  matrix products  10.4 us (2%)
    psum x1, blocking collectives, shards(): lax.psum((jnp.sum(out_wide, axis=1), jnp.sum(out_wide * out_wide, axis=1)...  138 us
    unnamed x9, waiting for transfers between devices  82.4 us
    all_to_all x1, waiting for transfers between devices, shards(): lax.all_to_all(outputs.reshape(group_count, row_total, head_count, HD), '...  45.9 us
    all_gather x2, blocking collectives, combined_all(): everything = jax.tree.map(lambda part: lax.all_gather(part, axis), shard)  45.5 us
    reduce_scatter x1, waiting for transfers between devices, shards(): lax.psum_scatter(jnp.dot(normed_a, up_weight, preferred_element_type=jnp....  38.8 us
    all_gather x1, waiting for transfers between devices, shards(): everyone = lax.all_gather(fresh_qkv[:, :, 0], 'pages', axis=0, tiled=True)  35.9 us
    all_gather x1, blocking collectives, shards(): lax.all_gather(hidden_two, 'row', axis=1, tiled=True)  24.8 us
    psum x1, blocking collectives, shards(): lax.psum(lax.psum((jnp.sum(hidden_one, axis=1), jnp.sum(hidden_one * hidd...  18.1 us
  transfers between devices with their start and end apart: 9, of which 7 were waited for; matrix products, arithmetic and copies ran while one was open for 6% of the time, Pallas kernels for 0%

profile of v1, /device:TPU:2, one launch (start us, length us, event | category | flops | bytes accessed | tf_op | source)
XLA Modules:
  0.0 582.3 jit_solution(6258925706972936199)
XLA Ops:
  19.8 35.9 %all-gather.9.cloned.1.call-done = bf16[512,2,1,512]{3,1,2,0:T(2,128)(2,1)} async-done(((bf16[32,2,1,512]{3,1,2,0:T(2,128)(2,1)}), bf16[512,2,1,512]{3,1,2,0:T(2,128)(2,1)}) %all-gather.9.cloned.1.call-update) | async-done | bytes 1048592 | tf_op jit(solution)/shard_map/all_gather | solution.py:195
  64.1 2.0 gather_fusion.4
  75.7 2.5 multiply_add_fusion
  80.2 4.6 all-to-all-start
  84.8 2.9 fusion.4
  89.6 2.6 scatter_fusion.4
  95.9 7.2 %all-to-all-start.1 = ((f32[16,1,256]{2,1,0:T(1,128)}), f32[16,1,256]{2,1,0:T(1,128)S(1)}, u32[]{:S(2)}, u32[]{:S(2)}) async-start(f32[16,1,256]{2,1,0:T(1,128)} %reshape.385), calls=%async_computation.1 | async-start | bytes 32768 | tf_op jit(solution)/shard_map/all_to_all | solution.py:217
  103.2 6.1 %fusion.3 = f32[512,2,4,128]{3,2,1,0:T(4,128)} fusion(f32[512,2,4,128]{3,1,0,2:T(2,128)} %bitcast.146, f32[512,2,4,128]{3,2,1,0:T(4,128)S(1)} %scatter_fusion.5, f32[512,2,4]{2,1,0:T(2,128)} %bitcast.154, f32[512,2,4]{2,1,0:T(2,128)} %bitcast.153), kind=kLoop, calls=%fused_computation.22 | loop fusion | flops 1572864 | bytes 6324224 | tf_op jit(solution)/shard_map/add | solution.py:57
  110.8 5.7 all-to-all-start.2
  119.7 45.9 %all-to-all-done.2 = f32[16,64,4,128]{3,2,1,0:T(4,128)S(1)} async-done(((f32[16,64,4,128]{3,2,1,0:T(4,128)}), f32[16,64,4,128]{3,2,1,0:T(4,128)S(1)}, u32[]{:S(2)}, u32[]{:S(2)}) %all-to-all-start.2) | async-done | bytes 2097184 | tf_op jit(solution)/shard_map/all_to_all | solution.py:224
  165.7 2.9 multiply_reduce_fusion
  170.8 24.3 %all-gather.4 = f32[8,64,4]{1,2,0:T(4,128)S(1)} all-gather(f32[1,64,4]{1,2,0:T(4,128)S(1)} %copy.149), channel_id=3, replica_groups=mesh['pages'=16,'row'=8,'col'=4] {'row'}, dimensions={0}, use_global_device_ids=true | all-gather | bytes 9216 | tf_op jit(solution)/shard_map/all_gather | solution.py:18
  195.2 21.2 %all-gather.5 = f32[8,64,4]{1,2,0:T(4,128)S(1)} all-gather(f32[1,64,4]{1,2,0:T(4,128)S(1)} %copy.155), channel_id=4, replica_groups=mesh['pages'=16,'row'=8,'col'=4] {'row'}, dimensions={0}, use_global_device_ids=true | all-gather | bytes 9216 | tf_op jit(solution)/shard_map/all_gather | solution.py:18
  217.3 10.9 %while.19 = (s32[]{:T(128)}, f32[64,4]{0,1:T(4,128)S(1)}, f32[64,4]{0,1:T(4,128)S(1)}, f32[64,4,128]{2,1,0:T(4,128)S(1)}, f32[8,64,4]{1,2,0:T(4,128)S(1)}, /*ind...) while((s32[]{:T(128)}, f32[64,4]{0,1:T(4,128)S(1)}, ...), condition=%wide.region_14.15_spmd, body=%wide.region_13.14_spmd.sunk | while | flops 99845 | bytes 407703 | solution.py:24
  230.0 20.7 %reduce-scatter.13.cloned.1.call-done = f32[64,64]{1,0:T(8,128)} async-done(((f32[256,64]{1,0:T(8,128)}), f32[64,64]{1,0:T(8,128)}) %reduce-scatter.13.cloned.1.call-update) | async-done | bytes 16400
  251.7 9.4 %all-reduce.2 = (f32[64]{0:T(128)S(1)}, f32[64]{0:T(128)S(1)}) all-reduce(f32[64]{0:T(128)S(1)} %get-tuple-element.200, f32[64]{0:T(128)S(1)} %get-tuple-element.199), channel_id=1, replica_groups=mesh['pages'=16,'row'=8,'col'=4] {'col'}, use_global_device_ids=true, to_apply=%region_22.23 | all-reduce | flops 128 | bytes 1024 | tf_op jit(solution)/shard_map/psum | solution.py:273
  261.1 18.1 %all-reduce.1 = (f32[64]{0:T(128)S(1)}, f32[64]{0:T(128)S(1)}) all-reduce(f32[64]{0:T(128)S(1)} %get-tuple-element.223, f32[64]{0:T(128)S(1)} %get-tuple-element.224), channel_id=1, replica_groups=mesh['pages'=16,'row'=8,'col'=4] {'row'}, use_global_device_ids=true, to_apply=%region_23.24 | all-reduce | flops 128 | bytes 1024 | tf_op jit(solution)/shard_map/psum | solution.py:272
  279.4 10.7 %all_gather.37 = bf16[64,256]{0,1:T(8,128)(2,1)S(1)} all-gather(bf16[64,64]{0,1:T(8,128)(2,1)S(1)} %copy.179), channel_id=1, replica_groups=mesh['pages'=16,'row'=8,'col'=4] {'col'}, dimensions={1}, use_global_device_ids=true | all-gather | bytes 40960 | tf_op jit(solution)/shard_map/all_gather | solution.py:276
  291.3 38.8 %reduce-scatter.11.cloned.1.call-done = f32[64,256]{1,0:T(8,128)} async-done(((f32[64,2048]{1,0:T(8,128)}), f32[64,256]{1,0:T(8,128)}) %reduce-scatter.11.cloned.1.call-update) | async-done | bytes 65552 | tf_op jit(solution)/shard_map/reduce_scatter | solution.py:279
  331.0 24.8 %all_gather.38 = bf16[64,2048]{1,0:T(8,128)(2,1)S(1)} all-gather(bf16[64,256]{1,0:T(8,128)(2,1)S(1)} %fusion.32), channel_id=1, replica_groups=mesh['pages'=16,'row'=8,'col'=4] {'row'}, dimensions={1}, use_global_device_ids=true | all-gather | bytes 294912 | tf_op jit(solution)/shard_map/all_gather | solution.py:289
  357.0 22.6 %reduce-scatter.15.cloned.1.call-done = bf16[64,64]{1,0:T(8,128)(2,1)} async-done(((bf16[256,64]{1,0:T(8,128)(2,1)}), bf16[64,64]{1,0:T(8,128)(2,1)}) %reduce-scatter.15.cloned.1.call-update) | async-done | bytes 8208
  380.7 138.0 %all-reduce = (f32[32,2]{1,0:T(8,128)S(1)}, f32[64]{0:T(128)S(1)}, f32[64]{0:T(128)S(1)}) all-reduce(f32[32,2]{1,0:T(8,128)S(1)} %reshape.245, f32[64]{0:T(128)S(1)} %get-tuple-element.202, f32[64]{0:T(128)S(1)} %get-tuple-element.201), channel_id=1, replica_groups=mesh['pages'=16,'row'=8,'col'=4] {'row','col'}, use_global_device_ids=true, to_apply=%region_27.28 | all-reduce | flops 192 | bytes 1536 | tf_op jit(solution)/shard_map/psum | solution.py:303
  518.9 14.2 %all_gather.39 = bf16[64,256]{0,1:T(8,128)(2,1)S(1)} all-gather(bf16[64,64]{0,1:T(8,128)(2,1)S(1)} %copy.180), channel_id=1, replica_groups=mesh['pages'=16,'row'=8,'col'=4] {'col'}, dimensions={1}, use_global_device_ids=true | all-gather | bytes 40960 | tf_op jit(solution)/shard_map/all_gather | solution.py:311
  535.0 39.0 %reduce-scatter.17.cloned.1.call-done = bf16[192,64]{1,0:T(8,128)(2,1)} async-done(((bf16[1536,64]{1,0:T(8,128)(2,1)}), bf16[192,64]{1,0:T(8,128)(2,1)}) %reduce-scatter.17.cloned.1.call-update) | async-done | bytes 24592
  (238 shorter events, 67.3 us)
Async XLA Ops:
  7.2 282.9 %copy-start = (bf16[256,2048]{1,0:T(8,128)(2,1)S(1)}, bf16[256,2048]{1,0:T(8,128)(2,1)}, u32[]{:S(2)}) copy-start(bf16[256,2048]{1,0:T(8,128)(2,1)} %param.35) | copy-start | bytes 3145732
  7.2 48.5 %all-gather.9.cloned.1.call-start = ((), (), s32[]{:S(2)}) async-start(), calls=%async_computation.8 | async-start | bytes 1114112 | tf_op jit(solution)/shard_map/all_gather | solution.py:195
  14.7 55.4 %copy-start.19 = (s32[16]{0:T(128)}, s32[16]{0:T(128)S(1)}, u32[]{:S(2)}) copy-start(s32[16]{0:T(128)S(1)} %compare_select_fusion.1) | copy-start | bytes 196
  18.9 50.5 %copy-start.16 = (pred[16,16]{1,0:T(8,128)(4,1)}, pred[16,16]{1,0:T(8,128)(4,1)S(1)}, u32[]{:S(2)}) copy-start(pred[16,16]{1,0:T(8,128)(4,1)S(1)} %broadcast_compare_fusion.1) | copy-start | bytes 772
  80.2 15.7 %all-to-all-start = ((f32[16,1,256]{2,1,0:T(1,128)}), f32[16,1,256]{2,1,0:T(1,128)S(1)}, u32[]{:S(2)}, u32[]{:S(2)}) async-start(f32[16,1,256]{2,1,0:T(1,128)} %reshape.383), calls=%async_computation | async-start | bytes 32768 | tf_op jit(solution)/shard_map/all_to_all | solution.py:210
  95.9 14.9 %all-to-all-start.1 = ((f32[16,1,256]{2,1,0:T(1,128)}), f32[16,1,256]{2,1,0:T(1,128)S(1)}, u32[]{:S(2)}, u32[]{:S(2)}) async-start(f32[16,1,256]{2,1,0:T(1,128)} %reshape.385), calls=%async_computation.1 | async-start | bytes 32768 | tf_op jit(solution)/shard_map/all_to_all | solution.py:217
  110.8 54.9 %all-to-all-start.2 = ((f32[16,64,4,128]{3,2,1,0:T(4,128)}), f32[16,64,4,128]{3,2,1,0:T(4,128)S(1)}, u32[]{:S(2)}, u32[]{:S(2)}) async-start(f32[16,64,4,128]{3,2,1,0:T(4,128)} %bitcast.145), calls=%async_computation.2 | async-start | bytes 4194304 | tf_op jit(solution)/shard_map/all_to_all | solution.py:224
  116.5 52.1 %copy-start.8 = (bf16[32,2,3,512]{3,1,2,0:T(2,128)(2,1)S(1)}, bf16[32,2,3,512]{3,1,2,0:T(2,128)(2,1)}, u32[]{:S(2)}) copy-start(bf16[32,2,3,512]{3,1,2,0:T(2,128)(2,1)} %param.24) | copy-start | bytes 589828
  116.5 99.8 %all-gather.11.cloned.1.call-start = ((), (), s32[]{:S(2)}) async-start(), calls=%async_computation.9 | async-start | bytes 1179648 | tf_op jit(solution)/shard_map/all_gather | solution.py:18
  118.7 50.2 %copy-start.35 = (f32[4]{0:T(128)S(1)}, f32[4]{0:T(128)}, u32[]{:S(2)}) copy-start(f32[4]{0:T(128)} %multiply_exponential_fusion) | copy-start | bytes 52
  168.6 82.1 %reduce-scatter.13.cloned.1.call-start = ((), (), s32[]{:S(2)}) async-start(), calls=%async_computation.10 | async-start | bytes 163840
  170.5 58.4 %copy-start.9 = (bf16[512,256]{1,0:T(8,128)(2,1)S(1)}, bf16[512,256]{1,0:T(8,128)(2,1)}, u32[]{:S(2)}) copy-start(bf16[512,256]{1,0:T(8,128)(2,1)} %param.31) | copy-start | bytes 786436
  228.2 63.0 %copy-start.31 = (bf16[64]{0:T(256)(128)(2,1)S(1)}, bf16[64]{0:T(256)(128)(2,1)}, u32[]{:S(2)}) copy-start(bf16[64]{0:T(256)(128)(2,1)} %param.38) | copy-start | bytes 388
  228.2 63.0 %copy-start.32 = (bf16[256]{0:T(256)(128)(2,1)S(1)}, bf16[256]{0:T(256)(128)(2,1)}, u32[]{:S(2)}) copy-start(bf16[256]{0:T(256)(128)(2,1)} %param.36) | copy-start | bytes 1540
  228.3 63.0 %copy-start.28 = (bf16[256]{0:T(256)(128)(2,1)S(1)}, bf16[256]{0:T(256)(128)(2,1)}, u32[]{:S(2)}) copy-start(bf16[256]{0:T(256)(128)(2,1)} %param.40) | copy-start | bytes 1540
  228.3 63.0 %copy-start.29 = (bf16[256]{0:T(256)(128)(2,1)S(1)}, bf16[256]{0:T(256)(128)(2,1)}, u32[]{:S(2)}) copy-start(bf16[256]{0:T(256)(128)(2,1)} %param.39) | copy-start | bytes 1540
  228.3 127.6 %copy-start.4 = (bf16[2048,256]{1,0:T(8,128)(2,1)S(1)}, bf16[2048,256]{1,0:T(8,128)(2,1)}, u32[]{:S(2)}) copy-start(bf16[2048,256]{1,0:T(8,128)(2,1)} %param.37) | copy-start | bytes 3145732
  229.9 100.3 %reduce-scatter.11.cloned.1.call-start = ((), (), s32[]{:S(2)}) async-start(), calls=%async_computation.7 | async-start | bytes 589824 | tf_op jit(solution)/shard_map/reduce_scatter | solution.py:279
  279.3 77.7 %copy-start.33 = (bf16[256]{0:T(256)(128)(2,1)S(1)}, bf16[256]{0:T(256)(128)(2,1)}, u32[]{:S(2)}) copy-start(bf16[256]{0:T(256)(128)(2,1)} %param.41) | copy-start | bytes 1540
  290.0 243.1 %copy-start.5 = (bf16[256,1536]{1,0:T(8,128)(2,1)S(1)}, bf16[256,1536]{1,0:T(8,128)(2,1)}, u32[]{:S(2)}) copy-start(bf16[256,1536]{1,0:T(8,128)(2,1)} %param.42) | copy-start | bytes 2359300
  291.2 88.5 %reduce-scatter.15.cloned.1.call-start = ((), (), s32[]{:S(2)}) async-start(), calls=%async_computation.11 | async-start | bytes 81920
  331.0 203.3 %copy-start.34 = (bf16[192]{0:T(256)(128)(2,1)S(1)}, bf16[192]{0:T(256)(128)(2,1)}, u32[]{:S(2)}) copy-start(bf16[192]{0:T(256)(128)(2,1)} %param.43) | copy-start | bytes 1156
  356.9 217.1 %reduce-scatter.17.cloned.1.call-start = ((), (), s32[]{:S(2)}) async-start(), calls=%async_computation.12 | async-start | bytes 442368
  380.6 194.9 %copy-start.15 = (bf16[64,64]{1,0:T(8,128)(2,1)}, bf16[64,64]{1,0:T(8,128)(2,1)S(1)}, u32[]{:S(2)}) copy-start(bf16[64,64]{1,0:T(8,128)(2,1)S(1)} %get-tuple-element.229) | copy-start | bytes 24580
  (21 other events, 209.7 us)
Sparse Core Ops, SparseCore 0:
  10.2 45.4 all-gather.8
  168.7 41.4 all-gather.10
  230.0 20.6 reduce-scatter.12
  291.3 38.8 reduce-scatter.10
  357.0 22.5 reduce-scatter.14
  534.5 39.4 reduce-scatter.16
